TPU v7x, 256 devices: a whole 4x4x8 slice. The times are simulated.
256 devices in a mesh: hid: 32 (over y, z), wid: 4 (over x), ad: 2 (over core).
Axes of the slice: x: 4, y: 4, z: 8, core: 2. Of those that a mesh axis runs over, the one named last changes fastest.
Arguments:
- activations: bfloat16 [1536, 2, 8192], P(None, None, ('wid', 'ad')), may hold values from -6 to 6
- row_adapter_index: int32 [1536, 2], replicated, may hold values from 0 to 127, as said below
- gate_up_weight: bfloat16 [8192, 2, 14848], P(('wid', 'ad'), None, 'hid'), may hold values from -0.0625 to 0.0625
- down_weight: bfloat16 [14848, 8192], P('hid', ('wid', 'ad')), may hold values from -0.046875 to 0.046875
- adapter_shrink_weight: bfloat16 [128, 2, 64, 8192], P(('hid', 'wid'), 'ad'), may hold values from -0.0625 to 0.0625
- adapter_expand_weight: bfloat16 [128, 2, 64, 14848], P(('hid', 'wid'), 'ad'), may hold values from -0.75 to 0.75
Outputs:
- layer_out: bfloat16 [1536, 2, 8192], P('hid', None, ('wid', 'ad'))
Inputs may be any that keep to these rules, and one draw needn't show every extreme that they name: `row_adapter_index`: call rows 48 * h to 48 * h + 47 of both batches together block h. In every block no adapter is named more than 2 times, and one and the same adapter is named exactly 2 times in every block.
All inputs are finite; a program needn't handle non-finite values.
Results may differ from a plain program's by a relative error of at most 0.0064.
Values may be sent and summed in bfloat16 or wider, within the bound.
No kernel may reach another device: no remote copies, remote signals or barrier semaphores. Data moves between devices by JAX's collectives and lax.ppermute only.
A program may use at most 128 MiB of HBM per device.

v0:
```python
import jax
import jax.numpy as jnp
from jax import lax
from jax.sharding import PartitionSpec as P


def slot_targets(block_ids, wid_count, wid_index, hid_count, group_capacity):
    row_count = block_ids.shape[1]
    matches = block_ids[:, :, None] == block_ids[:, None, :]
    earlier = jnp.arange(row_count)[None, :] < jnp.arange(row_count)[:, None]
    row_rank = jnp.sum(jnp.logical_and(matches, earlier[None]).astype(jnp.int32), axis=2)
    owner_hid = block_ids // wid_count
    is_mine = block_ids % wid_count == wid_index
    return jnp.where(is_mine, owner_hid * group_capacity + row_rank, hid_count * group_capacity)


def process_group(
    activations,
    row_adapter_index,
    gate_up_weight,
    down_weight,
    adapter_shrink_weight,
    adapter_expand_weight,
    group_capacity,
):
    hid_count = lax.axis_size("hid")
    wid_count = lax.axis_size("wid")
    hid_index = lax.axis_index("hid")
    wid_index = lax.axis_index("wid")
    proj_index = lax.axis_index("ad")
    total_rows, batch_count, local_width = activations.shape
    block_rows = total_rows // hid_count
    flat_width = block_rows * batch_count
    ff_local = down_weight.shape[0]
    own_rows = lax.dynamic_slice_in_dim(activations, hid_index * block_rows, block_rows, 0)
    full_rows = lax.all_gather(own_rows, ("wid", "ad"), axis=2, tiled=True)
    full_rows = full_rows.reshape(flat_width, -1)
    block_ids = row_adapter_index.reshape(hid_count, flat_width)
    targets = slot_targets(block_ids, wid_count, wid_index, hid_count, group_capacity)
    own_targets = lax.dynamic_index_in_dim(targets, hid_index, 0, keepdims=False)
    send_rows = jnp.zeros((hid_count * group_capacity, full_rows.shape[1]), full_rows.dtype)
    send_rows = (
        send_rows.at[own_targets].set(full_rows, mode="drop").reshape(hid_count, group_capacity, -1)
    )
    shrink_weight = adapter_shrink_weight[0, 0]
    expand_weight = adapter_expand_weight[0, 0]
    rank_values = jnp.einsum(
        "hcd,rd->hcr",
        lax.all_to_all(send_rows, "hid", split_axis=0, concat_axis=0, tiled=True),
        shrink_weight,
        preferred_element_type=jnp.float32,
    ).astype(jnp.bfloat16)
    deltas = jnp.einsum(
        "hcr,rf->hcf", rank_values, expand_weight, preferred_element_type=jnp.float32
    ).astype(jnp.bfloat16)
    deltas = deltas.reshape(hid_count, group_capacity, hid_count, ff_local)
    returned = lax.all_to_all(deltas, "hid", split_axis=2, concat_axis=2, tiled=True)
    row_slot = targets % group_capacity
    owner_slot = targets // group_capacity
    slot_total = hid_count * group_capacity * hid_count
    positions = (
        jnp.arange(hid_count, dtype=jnp.int32)[:, None] * group_capacity + row_slot
    ) * hid_count + owner_slot
    positions = jnp.where(targets < hid_count * group_capacity, positions, slot_total)
    flat_rows = (
        jnp.arange(hid_count, dtype=jnp.int32)[:, None] * flat_width
        + jnp.arange(flat_width, dtype=jnp.int32)[None, :]
    )
    slot_rows = jnp.full((slot_total,), total_rows * batch_count, jnp.int32)
    slot_rows = slot_rows.at[positions.reshape(-1)].set(flat_rows.reshape(-1), mode="drop")
    acts_flat = activations.reshape(total_rows * batch_count, local_width)
    weights = gate_up_weight.reshape(gate_up_weight.shape[0], -1)
    partial_value = jnp.dot(acts_flat, weights, preferred_element_type=jnp.float32).reshape(
        -1, 2, ff_local
    )
    partial_value = partial_value.at[slot_rows, proj_index].add(
        returned.reshape(-1, ff_local).astype(jnp.float32), mode="drop"
    )
    summed = lax.psum(partial_value, ("wid", "ad"))
    hidden = (jax.nn.silu(summed[:, 0]) * summed[:, 1]).astype(jnp.bfloat16)
    hidden_rows3 = hidden.reshape(total_rows, batch_count, ff_local)
    result = lax.psum_scatter(
        jnp.einsum("rbf,fd->rbd", hidden_rows3, down_weight, preferred_element_type=jnp.float32),
        "hid",
        scatter_dimension=0,
        tiled=True,
    )
    return result.astype(jnp.bfloat16)


def local(
    activations,
    row_adapter_index,
    gate_up_weight,
    down_weight,
    adapter_shrink_weight,
    adapter_expand_weight,
):
    hid_count = lax.axis_size("hid")
    wid_count = lax.axis_size("wid")
    block_rows = activations.shape[0] // hid_count
    batch_total = activations.shape[1]
    group_capacity = max(2, 2 * batch_total * block_rows // (hid_count * wid_count))
    return process_group(
        activations,
        row_adapter_index,
        gate_up_weight,
        down_weight,
        adapter_shrink_weight,
        adapter_expand_weight,
        group_capacity,
    )


def solution(mesh):
    in_specs = (
        P(None, None, ("wid", "ad")),
        P(),
        P(("wid", "ad"), None, "hid"),
        P("hid", ("wid", "ad")),
        P(("hid", "wid"), "ad", None, None),
        P(("hid", "wid"), "ad", None, None),
    )
    out_specs = P("hid", None, ("wid", "ad"))
    return jax.shard_map(local, mesh=mesh, in_specs=in_specs, out_specs=out_specs, check_vma=False)
```

profile of v0, /device:TPU:4, one launch (start us, length us, event | category | flops | bytes accessed | tf_op | source)
XLA Modules:
  0.0 711.8 jit_solution(1682355030441047729)
XLA Ops:
  6.5 0.0 all-gather.2.cloned.1.call-start
  6.5 1.9 constant_dynamic-slice_fusion.4
  8.4 0.0 all-gather.2.cloned.1.call-update
  8.4 1.0 copy.46
  9.4 0.3 eq.38
  9.8 1.2 convert_reduce_fusion
  11.1 28.2 %all-gather.2.cloned.1.call-done = bf16[48,2,8192]{2,1,0:T(2,128)(2,1)} async-done(((bf16[48,2,1024]{2,1,0:T(2,128)(2,1)}), bf16[48,2,8192]{2,1,0:T(2,128)(2,1)}) %all-gather.2.cloned.1.call-update) | async-done | bytes 1572880 | tf_op jit(solution)/shard_map/all_gather | solution.py:36
  39.3 3.7 reshape.318
  42.9 4.5 scatter_custom_fusion.1
  47.4 2.5 reshape.299
  49.9 39.0 %all_to_all.10 = bf16[32,2,8192]{2,1,0:T(2,128)(2,1)} all-to-all(bf16[32,2,8192]{2,1,0:T(2,128)(2,1)} %reshape.299), channel_id=1, replica_groups=mesh['hid'=32,'wid'=4,'ad'=2] {'hid'}, dimensions={0} | all-to-all | bytes 2097152 | tf_op jit(solution)/shard_map/all_to_all | solution.py:49
  88.9 5.1 convolution_convert_fusion
  94.0 6.6 reshape.300
  100.6 5.0 copy.49
  105.7 5.3 all-to-all-start.1
  110.9 0.2 all-reduce.3.cloned.1.call-start
  111.2 0.5 reshape.297
  111.6 0.1 reduce_sum.12
  111.7 10.2 %reshape.328 = bf16[3072,1024,1]{1,0,2:T(8,128)(2,1)} reshape(bf16[1536,2,1024]{2,1,0:T(2,128)(2,1)} %param.6) | data formatting | bytes 12582912 | tf_op jit(solution)/shard_map/reshape | solution.py:71
  121.9 0.1 iota_add_fusion
  122.0 0.1 reshape.310
  122.0 0.1 add.157
  122.1 0.1 add.158
  122.2 0.0 copy-done
  122.2 11.7 %fusion.5 = f32[3072,2,464]{0,2,1:T(8,128)} fusion(bf16[3072,1024,1]{1,0,2:T(8,128)(2,1)} %reshape.328, bf16[1024,2,464]{0,2,1:T(8,128)(2,1)S(1)} %copy-done), kind=kOutput, calls=%fused_computation.12 | convolution fusion | flops 5838471168 | bytes 19595264 | tf_op jit(solution)/shard_map/dot_general | solution.py:73
  134.0 18.8 %copy.45 = f32[3072,2,464]{2,1,0:T(2,128)} copy(f32[3072,2,464]{0,2,1:T(8,128)} %fusion.5) | data formatting | bytes 22806528 | tf_op jit(solution)/shard_map/dot_general | solution.py:73
  152.8 16.0 %reshape.302 = f32[6144,464]{1,0:T(8,128)} reshape(f32[3072,2,464]{2,1,0:T(2,128)} %copy.45) | data formatting | bytes 22806528
  168.7 0.2 compare_select_fusion
  169.0 11.8 %scatter_custom_fusion = s32[2048]{0:T(1024)S(1)} fusion(s32[3072]{0:T(1024)S(1)} %bitcast.37, s32[3072]{0:T(1024)S(1)} %reshape.310, s32[]{:T(128)} %constant.74.clone.1), kind=kCustom, calls=%fused_computation.45 | custom fusion | bytes 8196 | tf_op jit(solution)/shard_map/scatter | solution.py:70
  180.8 0.1 multiply_reduce_fusion
  180.9 0.1 and_reduce_fusion
  181.0 0.0 all-to-all-done.1
  181.0 4.7 copy.50
  185.7 22.4 %scatter_custom_fusion.2 = f32[6144,464]{1,0:T(8,128)} fusion(f32[6144,464]{1,0:T(8,128)} %reshape.302, s32[2048]{0:T(1024)S(1)} %broadcast_select_fusion, bf16[2048,464]{1,0:T(8,128)(2,1)} %bitcast.34), kind=kCustom, calls=%fused_computation.7 | custom fusion | flops 1900544 | bytes 13500416
  208.1 15.5 %reshape.303 = f32[3072,2,464]{2,1,0:T(2,128)} reshape(f32[6144,464]{1,0:T(8,128)} %scatter_custom_fusion.2) | data formatting | bytes 22806528 | tf_op jit(solution)/shard_map/scatter-add | solution.py:76
  223.6 0.0 all-reduce.3.cloned.1.call-update
  223.6 0.3 reduce-scatter.2.cloned.1.call-start
  223.9 147.6 %all-reduce.3.cloned.1.call-done = f32[3072,2,464]{2,1,0:T(2,128)} async-done(((f32[3072,2,464]{2,1,0:T(2,128)}), f32[3072,2,464]{2,1,0:T(2,128)}) %all-reduce.3.cloned.1.call-update) | async-done | bytes 11403280 | tf_op jit(solution)/shard_map/psum | solution.py:79
  371.6 42.2 %slice_reduce_fusion.1 = (f32[3072,464]{1,0:T(8,128)}, f32[3072,464]{1,0:T(8,128)}) fusion(f32[3072,2,464]{2,1,0:T(2,128)} %all-reduce.3.cloned.1.call-done), kind=kLoop, calls=%fused_computation.5 | loop fusion | bytes 22806528 | tf_op jit(solution)/shard_map/slice | solution.py:80
  413.8 8.4 %squeeze.19 = f32[1536,2,464]{2,1,0:T(2,128)} reshape(f32[3072,464]{1,0:T(8,128)} %get-tuple-element.5) | data formatting | bytes 11403264 | tf_op jit(solution)/shard_map/squeeze | solution.py:80
  422.2 10.2 %copy.52 = f32[1536,2,464]{0,2,1:T(8,128)} copy(f32[1536,2,464]{2,1,0:T(2,128)} %squeeze.19) | data formatting | bytes 11403264 | tf_op jit(solution)/shard_map/squeeze | solution.py:80
  432.4 8.4 %squeeze.20 = f32[1536,2,464]{2,1,0:T(2,128)} reshape(f32[3072,464]{1,0:T(8,128)} %get-tuple-element.6) | data formatting | bytes 11403264 | tf_op jit(solution)/shard_map/squeeze | solution.py:80
  440.8 10.3 %copy.53 = f32[1536,2,464]{0,2,1:T(8,128)} copy(f32[1536,2,464]{2,1,0:T(2,128)} %squeeze.20) | data formatting | bytes 11403264 | tf_op jit(solution)/shard_map/squeeze | solution.py:80
  451.1 10.9 %fusion.2 = f32[1536,2,1024]{2,0,1:T(8,128)} fusion(f32[1536,2,464]{0,2,1:T(8,128)} %copy.53, f32[1536,2,464]{0,2,1:T(8,128)} %copy.52, bf16[464,1024]{1,0:T(8,128)(2,1)S(1)} %copy-done.4), kind=kOutput, calls=%fused_computation.9 | convolution fusion | flops 2927788032 | bytes 24936448 | tf_op jit(solution)/shard_map/rbf,fd->rbd/dot_general | solution.py:83
  462.0 0.0 reduce-scatter.2.cloned.1.call-update
  462.1 241.3 %reduce-scatter.2.cloned.1.call-done = f32[48,2,1024]{2,0,1:T(8,128)} async-done(((f32[1536,2,1024]{2,0,1:T(8,128)}), f32[48,2,1024]{2,0,1:T(8,128)}) %reduce-scatter.2.cloned.1.call-update) | async-done | bytes 393232 | tf_op jit(solution)/shard_map/reduce_scatter | solution.py:82
  703.4 1.0 convert_element_type.28
  704.4 0.9 copy.54
  (17 shorter events, 0.1 us)
Async XLA Ops:
  6.5 115.7 %copy-start = (bf16[1024,2,464]{0,2,1:T(8,128)(2,1)S(1)}, bf16[1024,2,464]{0,2,1:T(8,128)(2,1)}, u32[]{:S(2)}) copy-start(bf16[1024,2,464]{0,2,1:T(8,128)(2,1)} %param.8) | copy-start | bytes 5701636
  6.5 32.7 %all-gather.2.cloned.1.call-start = ((), (), s32[]{:S(2)}) async-start(), calls=%async_computation.3 | async-start | bytes 1769472 | tf_op jit(solution)/shard_map/all_gather | solution.py:36
  105.7 75.3 %all-to-all-start.1 = ((bf16[32,2,32,464]{3,1,0,2:T(2,128)(2,1)}), bf16[32,2,32,464]{3,1,0,2:T(2,128)(2,1)}, u32[]{:S(2)}, u32[]{:S(2)}) async-start(bf16[32,2,32,464]{3,1,0,2:T(2,128)(2,1)} %copy.49), calls=%async_computation.1 | async-start | bytes 4194304 | tf_op jit(solution)/shard_map/all_to_all | solution.py:57
  110.9 260.6 %all-reduce.3.cloned.1.call-start = ((), (), s32[]{:S(2)}) async-start(), calls=%async_computation.4 | async-start | bytes 25165824 | tf_op jit(solution)/shard_map/psum | solution.py:79
  152.8 28.0 %copy-start.3 = (s32[2]{0:T(128)S(1)}, s32[2]{0:T(128)}, u32[]{:S(2)}) copy-start(s32[2]{0:T(128)} %constant.98) | copy-start | bytes 28
  152.8 28.1 %copy-start.2 = (s32[2]{0:T(128)S(1)}, s32[2]{0:T(128)}, u32[]{:S(2)}) copy-start(s32[2]{0:T(128)} %constant.101) | copy-start | bytes 28
  223.6 479.8 %reduce-scatter.2.cloned.1.call-start = ((), (), s32[]{:S(2)}) async-start(), calls=%async_computation.5 | async-start | bytes 12976128 | tf_op jit(solution)/shard_map/reduce_scatter | solution.py:82
  440.8 10.3 %copy-start.4 = (bf16[464,1024]{1,0:T(8,128)(2,1)S(1)}, bf16[464,1024]{1,0:T(8,128)(2,1)}, u32[]{:S(2)}) copy-start(bf16[464,1024]{1,0:T(8,128)(2,1)} %param.9) | copy-start | bytes 2850820
  462.0 243.3 %copy-start.1 = (bf16[1024,2,464]{0,2,1:T(8,128)(2,1)S(1)}, bf16[1024,2,464]{0,2,1:T(8,128)(2,1)}, u32[]{:S(2)}) copy-start(bf16[1024,2,464]{0,2,1:T(8,128)(2,1)} %param.8) | copy-start | bytes 5701636
Sparse Core Ops, SparseCore 0:
  9.2 30.0 all-gather.1
  223.8 147.7 all-reduce.2
  462.2 241.1 reduce-scatter.1
where the time goes:
time: 715 us; the launch traced here: 712 us
  waiting for transfers between devices  417 us (58%)
  local copies, waits for them, and re-layouts  184 us (26%)
  blocking collectives  39 us (5%)
  matrix products  27.8 us (4%)
  other arithmetic  25.2 us (4%)
  between operations  13.3 us (2%)
    reduce_scatter x1, waiting for transfers between devices, process_group(): lax.psum_scatter(jnp.einsum('rbf,fd->rbd', hidden_rows3, down_weight, pre...  241 us
    psum x1, waiting for transfers between devices, process_group(): summed = lax.psum(partial_value, ('wid', 'ad'))  148 us
    slice x1, local copies, waits for them, and re-layouts, process_group(): hidden = (jax.nn.silu(summed[:, 0]) * summed[:, 1]).astype(jnp.bfloat16)  42.2 us
    all_to_all x1, blocking collectives, process_group(): lax.all_to_all(send_rows, 'hid', split_axis=0, concat_axis=0, tiled=True)  39 us
    squeeze x4, local copies, waits for them, and re-layouts, process_group(): hidden = (jax.nn.silu(summed[:, 0]) * summed[:, 1]).astype(jnp.bfloat16)  37.3 us
    all_gather x1, waiting for transfers between devices, process_group(): full_rows = lax.all_gather(own_rows, ('wid', 'ad'), axis=2, tiled=True)  28.2 us
    unnamed x4, other arithmetic  22.6 us
    dot_general x1, local copies, waits for them, and re-layouts, process_group(): jnp.dot(acts_flat, weights, preferred_element_type=jnp.float32)  18.8 us
  transfers between devices with their start and end apart: 4, of which 3 were waited for; matrix products, arithmetic and copies ran while one was open for 10% of the time, Pallas kernels for 0%

commit v1 on v0

--- a/solution.py
+++ b/solution.py
@@ -76,7 +76,7 @@
     partial_value = partial_value.at[slot_rows, proj_index].add(
         returned.reshape(-1, ff_local).astype(jnp.float32), mode="drop"
     )
-    summed = lax.psum(partial_value, ("wid", "ad"))
+    summed = jnp.sum(lax.all_gather(partial_value, ("wid", "ad")), axis=0)
     hidden = (jax.nn.silu(summed[:, 0]) * summed[:, 1]).astype(jnp.bfloat16)
     hidden_rows3 = hidden.reshape(total_rows, batch_count, ff_local)
     result = lax.psum_scatter(

time: 715 us -> 1000 us (1.40)
  waiting for transfers between devices: 417 us -> 669 us
  other arithmetic: 25.2 us -> 58.2 us
    all_gather x0 -> x1, waiting for transfers between devices: none -> 400 us  [process_group(): summed = jnp.sum(lax.all_gather(partial_value, ('wid', 'ad')), axis=0)]
    psum x1 -> x0, waiting for transfers between devices: 148 us -> none  [process_group(): summed = lax.psum(partial_value, ('wid', 'ad'))]
    all_gather x0 -> x2, local copies, waits for them, and re-layouts: none -> 34.5 us  [process_group(): summed = jnp.sum(lax.all_gather(partial_value, ('wid', 'ad')), axis=0)]
    reduce_sum x0 -> x1, other arithmetic: none -> 33 us  [process_group(): summed = jnp.sum(lax.all_gather(partial_value, ('wid', 'ad')), axis=0)]
    slice x1, local copies, waits for them, and re-layouts: 42.2 us -> 9.92 us  [process_group(): hidden = (jax.nn.silu(summed[:, 0]) * summed[:, 1]).astype(jnp.bfloat16)]
    scatter-add x1 -> x0, local copies, waits for them, and re-layouts: 15.5 us -> none  [process_group(): partial_value.at[slot_rows, proj_index]]
    unnamed x12 -> x14, local copies, waits for them, and re-layouts: 17 us -> 29.8 us
  transfers between devices with their start and end apart: 4 -> 4, of which waited for: 3 -> 3; matrix products, arithmetic and copies ran while one was open for 10% -> 7% of each run, Pallas kernels for 0% -> 0%
where the time goes in v1:
time: 1000 us; the launch traced here: 996 us
  waiting for transfers between devices  669 us (67%)
  local copies, waits for them, and re-layouts  183 us (18%)
  other arithmetic  58.2 us (6%)
  blocking collectives  39 us (4%)
  matrix products  27.8 us (3%)
  between operations  13.3 us (1%)
    all_gather x1, waiting for transfers between devices, process_group(): summed = jnp.sum(lax.all_gather(partial_value, ('wid', 'ad')), axis=0)  400 us
    reduce_scatter x1, waiting for transfers between devices, process_group(): lax.psum_scatter(jnp.einsum('rbf,fd->rbd', hidden_rows3, down_weight, pre...  241 us
    all_to_all x1, blocking collectives, process_group(): lax.all_to_all(send_rows, 'hid', split_axis=0, concat_axis=0, tiled=True)  39 us
    squeeze x4, local copies, waits for them, and re-layouts, process_group(): hidden = (jax.nn.silu(summed[:, 0]) * summed[:, 1]).astype(jnp.bfloat16)  37.2 us
    all_gather x2, local copies, waits for them, and re-layouts, process_group(): summed = jnp.sum(lax.all_gather(partial_value, ('wid', 'ad')), axis=0)  34.5 us
    reduce_sum x1, other arithmetic, process_group(): summed = jnp.sum(lax.all_gather(partial_value, ('wid', 'ad')), axis=0)  33 us
    unnamed x14, local copies, waits for them, and re-layouts  29.8 us
    all_gather x1, waiting for transfers between devices, process_group(): full_rows = lax.all_gather(own_rows, ('wid', 'ad'), axis=2, tiled=True)  28.2 us
  transfers between devices with their start and end apart: 4, of which 3 were waited for; matrix products, arithmetic and copies ran while one was open for 7% of the time, Pallas kernels for 0%

profile of v1, /device:TPU:4, one launch (start us, length us, event | category | flops | bytes accessed | tf_op | source)
XLA Modules:
  0.0 996.1 jit_solution(4449954403367666932)
XLA Ops:
  6.5 1.9 constant_dynamic-slice_fusion.4
  8.4 0.0 all-gather.3.cloned.1.call-update
  8.4 1.0 copy.54
  9.4 0.3 eq.38
  9.8 1.2 convert_reduce_fusion
  11.1 28.2 %all-gather.3.cloned.1.call-done = bf16[48,2,8192]{2,1,0:T(2,128)(2,1)} async-done(((bf16[48,2,1024]{2,1,0:T(2,128)(2,1)}), bf16[48,2,8192]{2,1,0:T(2,128)(2,1)}) %all-gather.3.cloned.1.call-update) | async-done | bytes 1572880 | tf_op jit(solution)/shard_map/all_gather | solution.py:36
  39.3 3.7 reshape.319
  42.9 4.5 scatter_custom_fusion.1
  47.4 2.5 reshape.299
  49.9 39.0 %all_to_all.10 = bf16[32,2,8192]{2,1,0:T(2,128)(2,1)} all-to-all(bf16[32,2,8192]{2,1,0:T(2,128)(2,1)} %reshape.299), channel_id=1, replica_groups=mesh['hid'=32,'wid'=4,'ad'=2] {'hid'}, dimensions={0} | all-to-all | bytes 2097152 | tf_op jit(solution)/shard_map/all_to_all | solution.py:49
  88.9 5.1 convolution_convert_fusion
  94.0 6.6 reshape.300
  100.6 5.0 copy.57
  105.7 5.3 all-to-all-start.1
  110.9 0.2 all-gather.5.cloned.1.call-start
  111.2 0.5 reshape.297
  111.6 0.1 reduce_sum.21
  111.7 10.2 %reshape.329 = bf16[3072,1024,1]{1,0,2:T(8,128)(2,1)} reshape(bf16[1536,2,1024]{2,1,0:T(2,128)(2,1)} %param.6) | data formatting | bytes 12582912 | tf_op jit(solution)/shard_map/reshape | solution.py:71
  121.9 0.1 iota_add_fusion
  122.0 0.1 reshape.311
  122.0 0.1 add.155
  122.1 0.1 add.156
  122.2 11.7 %fusion.5 = f32[3072,2,464]{0,2,1:T(8,128)} fusion(bf16[3072,1024,1]{1,0,2:T(8,128)(2,1)} %reshape.329, bf16[1024,2,464]{0,2,1:T(8,128)(2,1)S(1)} %copy-done), kind=kOutput, calls=%fused_computation.12 | convolution fusion | flops 5838471168 | bytes 19595264 | tf_op jit(solution)/shard_map/dot_general | solution.py:73
  134.0 18.8 %copy.53 = f32[3072,2,464]{2,1,0:T(2,128)} copy(f32[3072,2,464]{0,2,1:T(8,128)} %fusion.5) | data formatting | bytes 22806528 | tf_op jit(solution)/shard_map/dot_general | solution.py:73
  152.8 16.0 %reshape.302 = f32[6144,464]{1,0:T(8,128)} reshape(f32[3072,2,464]{2,1,0:T(2,128)} %copy.53) | data formatting | bytes 22806528
  168.7 0.2 compare_select_fusion
  169.0 11.8 %scatter_custom_fusion = s32[2048]{0:T(1024)S(1)} fusion(s32[3072]{0:T(1024)S(1)} %bitcast.41, s32[3072]{0:T(1024)S(1)} %reshape.311, s32[]{:T(128)} %constant.75.clone.1), kind=kCustom, calls=%fused_computation.45 | custom fusion | bytes 8196 | tf_op jit(solution)/shard_map/scatter | solution.py:70
  180.8 0.1 multiply_reduce_fusion
  180.9 0.1 and_reduce_fusion
  181.0 4.7 copy.58
  185.7 22.4 %scatter_custom_fusion.2 = f32[6144,464]{1,0:T(8,128)} fusion(f32[6144,464]{1,0:T(8,128)} %reshape.302, s32[2048]{0:T(1024)S(1)} %broadcast_select_fusion, bf16[2048,464]{1,0:T(8,128)(2,1)} %bitcast.38), kind=kCustom, calls=%fused_computation.7 | custom fusion | flops 1900544 | bytes 13500416
  208.1 15.5 %all_gather.10 = f32[1,3072,2,464]{3,2,1,0:T(2,128)} reshape(f32[6144,464]{1,0:T(8,128)} %scatter_custom_fusion.2) | data formatting | bytes 22806528 | tf_op jit(solution)/shard_map/all_gather | solution.py:79
  223.6 19.0 %copy.59 = f32[1,3072,2,464]{1,3,2,0:T(8,128)} copy(f32[1,3072,2,464]{3,2,1,0:T(2,128)} %all_gather.10) | data formatting | bytes 22806528 | tf_op jit(solution)/shard_map/all_gather | solution.py:79
  242.6 0.0 all-gather.5.cloned.1.call-update
  242.6 0.3 reduce-scatter.2.cloned.1.call-start
  242.9 400.2 %all-gather.5.cloned.1.call-done = f32[8,3072,2,464]{1,3,2,0:T(8,128)} async-done(((f32[1,3072,2,464]{1,3,2,0:T(8,128)}), f32[8,3072,2,464]{1,3,2,0:T(8,128)}) %all-gather.5.cloned.1.call-update) | async-done | bytes 91226128 | tf_op jit(solution)/shard_map/all_gather | solution.py:79
  643.1 33.0 %reduce_sum.22 = f32[3072,2,464]{0,2,1:T(8,128)} reduce(f32[8,3072,2,464]{1,3,2,0:T(8,128)} %all-gather.5.cloned.1.call-done, f32[]{:T(128)} %constant.92.clone.1), dimensions={0}, to_apply=%region_4.5 | reduce | flops 19955712 | bytes 102629376 | tf_op jit(solution)/shard_map/reduce_sum | solution.py:79
  676.1 9.9 slice_bitcast_fusion.1
  686.1 6.4 copy.72
  692.5 8.4 squeeze.19
  700.9 10.2 %copy.62 = f32[1536,2,464]{0,2,1:T(8,128)} copy(f32[1536,2,464]{2,1,0:T(2,128)} %squeeze.19) | data formatting | bytes 11403264 | tf_op jit(solution)/shard_map/squeeze | solution.py:80
  711.0 6.4 copy.73
  717.4 8.4 squeeze.20
  725.8 10.3 %copy.63 = f32[1536,2,464]{0,2,1:T(8,128)} copy(f32[1536,2,464]{2,1,0:T(2,128)} %squeeze.20) | data formatting | bytes 11403264 | tf_op jit(solution)/shard_map/squeeze | solution.py:80
  736.1 10.9 %fusion.2 = f32[1536,2,1024]{2,0,1:T(8,128)} fusion(f32[1536,2,464]{0,2,1:T(8,128)} %copy.63, f32[1536,2,464]{0,2,1:T(8,128)} %copy.62, bf16[464,1024]{1,0:T(8,128)(2,1)S(1)} %copy-done.4), kind=kOutput, calls=%fused_computation.9 | convolution fusion | flops 2927788032 | bytes 24936448 | tf_op jit(solution)/shard_map/rbf,fd->rbd/dot_general | solution.py:83
  747.1 240.6 %reduce-scatter.2.cloned.1.call-done = f32[48,2,1024]{2,0,1:T(8,128)} async-done(((f32[1536,2,1024]{2,0,1:T(8,128)}), f32[48,2,1024]{2,0,1:T(8,128)}) %reduce-scatter.2.cloned.1.call-update) | async-done | bytes 393232 | tf_op jit(solution)/shard_map/reduce_scatter | solution.py:82
  987.7 1.0 convert_element_type.28
  988.7 0.9 copy.64
  (21 shorter events, 0.1 us)
Async XLA Ops:
  6.5 115.7 %copy-start = (bf16[1024,2,464]{0,2,1:T(8,128)(2,1)S(1)}, bf16[1024,2,464]{0,2,1:T(8,128)(2,1)}, u32[]{:S(2)}) copy-start(bf16[1024,2,464]{0,2,1:T(8,128)(2,1)} %param.8) | copy-start | bytes 5701636
  6.5 32.7 %all-gather.3.cloned.1.call-start = ((), (), s32[]{:S(2)}) async-start(), calls=%async_computation.3 | async-start | bytes 1769472 | tf_op jit(solution)/shard_map/all_gather | solution.py:36
  105.7 75.3 %all-to-all-start.1 = ((bf16[32,2,32,464]{3,1,0,2:T(2,128)(2,1)}), bf16[32,2,32,464]{3,1,0,2:T(2,128)(2,1)}, u32[]{:S(2)}, u32[]{:S(2)}) async-start(bf16[32,2,32,464]{3,1,0,2:T(2,128)(2,1)} %copy.57), calls=%async_computation.1 | async-start | bytes 4194304 | tf_op jit(solution)/shard_map/all_to_all | solution.py:57
  110.9 532.2 %all-gather.5.cloned.1.call-start = ((), (), s32[]{:S(2)}) async-start(), calls=%async_computation.4 | async-start | bytes 102629376 | tf_op jit(solution)/shard_map/all_gather | solution.py:79
  152.8 28.0 %copy-start.3 = (s32[2]{0:T(128)S(1)}, s32[2]{0:T(128)}, u32[]{:S(2)}) copy-start(s32[2]{0:T(128)} %constant.100) | copy-start | bytes 28
  152.8 28.1 %copy-start.2 = (s32[2]{0:T(128)S(1)}, s32[2]{0:T(128)}, u32[]{:S(2)}) copy-start(s32[2]{0:T(128)} %constant.103) | copy-start | bytes 28
  242.6 745.1 %reduce-scatter.2.cloned.1.call-start = ((), (), s32[]{:S(2)}) async-start(), calls=%async_computation.5 | async-start | bytes 12976128 | tf_op jit(solution)/shard_map/reduce_scatter | solution.py:82
  725.8 10.3 %copy-start.4 = (bf16[464,1024]{1,0:T(8,128)(2,1)S(1)}, bf16[464,1024]{1,0:T(8,128)(2,1)}, u32[]{:S(2)}) copy-start(bf16[464,1024]{1,0:T(8,128)(2,1)} %param.9) | copy-start | bytes 2850820
  747.0 242.5 %copy-start.1 = (bf16[1024,2,464]{0,2,1:T(8,128)(2,1)S(1)}, bf16[1024,2,464]{0,2,1:T(8,128)(2,1)}, u32[]{:S(2)}) copy-start(bf16[1024,2,464]{0,2,1:T(8,128)(2,1)} %param.8) | copy-start | bytes 5701636
Sparse Core Ops, SparseCore 0:
  9.2 30.0 all-gather.2
  242.7 400.3 all-gather.4
  747.2 240.4 reduce-scatter.1
